TPU v7x, 256 devices: a whole 4x4x8 slice. The times are simulated.
256 devices in a mesh: freq: 16 (over z, core), seg: 16 (over x, y).
Axes of the slice: x: 4, y: 4, z: 8, core: 2. Of those that a mesh axis runs over, the one named last changes fastest.
Arguments:
- propagators: float32 [16, 256, 2, 128, 128], P('seg', 'freq'), may hold values from -2 to 2, as said below
- source_modes: float32 [256, 2, 128], P('freq'), may hold values from -6 to 6
Outputs:
- amplitudes: float32 [16, 256, 2, 128], P('seg', 'freq')
- waveforms: float32 [256, 16, 128], P('freq', 'seg')
Inputs may be any that keep to these rules, and one draw needn't show every extreme that they name: `propagators`: each propagator is a diagonal of unit phases times (the identity plus a dense complex coupling part).
All inputs are finite; a program needn't handle non-finite values.
Results may differ from a plain program's by a relative error of at most 0.00019.
Values sent between devices are 32-bit elements; how exact they have to be, the bound alone decides.
A program may use at most 64 MiB of HBM per device.

v0:
```python
import jax
import jax.numpy as jnp
from jax import lax
from jax.sharding import PartitionSpec as P


def split_up(array, dim, length):
    shape = array.shape
    pieces = array.reshape(*shape[:dim], length, shape[dim] // length, *shape[dim + 1 :])
    return jnp.moveaxis(pieces, dim, 0)


def sum_at_owner(array, axis, dim):
    pieces = split_up(array, dim, lax.axis_size(axis))
    arrived = lax.all_to_all(pieces, axis, split_axis=0, concat_axis=0, tiled=True)
    return arrived.sum(axis=0)


def apply_modes(prop, vec):
    hi = lax.Precision.HIGHEST
    real_part = jnp.einsum("fij,fj->fi", prop[:, 0], vec[:, 0], precision=hi) - jnp.einsum(
        "fij,fj->fi", prop[:, 1], vec[:, 1], precision=hi
    )
    imag_part = jnp.einsum("fij,fj->fi", prop[:, 0], vec[:, 1], precision=hi) + jnp.einsum(
        "fij,fj->fi", prop[:, 1], vec[:, 0], precision=hi
    )
    return jnp.stack([real_part, imag_part], axis=1)


def local(propagators, source_modes):
    own_prop = propagators[0]
    fr_count = own_prop.shape[0]
    seg_index = lax.axis_index("seg")
    seg_count = lax.axis_size("seg")
    group = (fr_count + seg_count - 1) // seg_count
    chain_props = lax.all_to_all(propagators, "seg", split_axis=1, concat_axis=0, tiled=True)
    my_src = lax.dynamic_slice_in_dim(source_modes, seg_index * group, group, 0)

    def advance(carry, prop):
        nxt = apply_modes(prop, carry)
        return (nxt, nxt)

    final_vec, chain_amps = lax.scan(advance, my_src, chain_props)
    returned = lax.all_to_all(chain_amps, "seg", split_axis=0, concat_axis=1, tiled=True)
    result = returned[0, :fr_count]
    total_times = lax.axis_size("freq") * fr_count
    freq_start = lax.axis_index("freq") * fr_count
    stacked = jnp.concatenate([result[:, 0], result[:, 1]], axis=0)
    scale = 1.0 / jnp.sqrt(jnp.float32(total_times))
    tgrid = jnp.arange(fr_count * lax.axis_size("freq"), dtype=jnp.int32)
    fgrid = freq_start + jnp.arange(fr_count, dtype=jnp.int32)
    phase = (tgrid[:, None] * fgrid[None, :] % total_times).astype(jnp.float32) * (
        2.0 * jnp.pi / total_times
    )
    table = jnp.concatenate([jnp.cos(phase), -jnp.sin(phase)], axis=1) * scale
    waveforms = sum_at_owner(
        jnp.dot(table, stacked, precision=lax.Precision.HIGHEST)[:, None, :], "freq", 0
    )
    return (result[None], waveforms)


def solution(mesh):
    placed = (P("seg", "freq", None, None, None), P("freq", None, None))
    return jax.shard_map(
        local,
        mesh=mesh,
        in_specs=placed,
        out_specs=(P("seg", "freq", None, None), P("freq", "seg", None)),
        check_vma=False,
    )
```

profile of v0, /device:TPU:1, one launch (start us, length us, event | category | flops | bytes accessed | tf_op | source)
XLA Modules:
  0.0 94.4 jit_solution(478646866631887296)
XLA Ops:
  0.6 7.6 %all-to-all-start = ((f32[1,16,2,128,128]{4,3,2,0,1:T(8,128)}), f32[1,16,2,128,128]{4,3,2,0,1:T(8,128)S(1)}, u32[]{:S(2)}, u32[]{:S(2)}) async-start(f32[1,16,2,128,128]{4,3,2,0,1:T(8,128)} %bitcast.95), calls=%async_computation | async-start | bytes 4194304 | tf_op jit(solution)/shard_map/all_to_all | solution.py:36
  8.3 27.8 %all-to-all-done = f32[1,16,2,128,128]{4,3,2,0,1:T(8,128)S(1)} async-done(((f32[1,16,2,128,128]{4,3,2,0,1:T(8,128)}), f32[1,16,2,128,128]{4,3,2,0,1:T(8,128)S(1)}, u32[]{:S(2)}, u32[]{:S(2)}) %all-to-all-start) | async-done | bytes 2097184 | tf_op jit(solution)/shard_map/all_to_all | solution.py:36
  36.1 23.7 %while.12 = (s32[]{:T(128)}, f32[1,2,128]{2,1,0:T(2,128)S(1)}, f32[16,1,2,128]{3,2,1,0:T(2,128)}, f32[16,1,2,128,128]{4,3,2,1,0:T(8,128)S(1)}, s32[]{:T(128)}) while((s32[]{:T(128)}, f32[1,2,128]{2,1,0:T(2,128)S(1)}, f32[16,1,2,128]{3,2,1,0:T(2,128)}, f32[16,1,2,128,128]{4,3,2,1,0:T(8,128)S(1)}, s32[]{:T(128)}) %tuple.33), condition=%wide.region_1.2_spmd, body=%wide.region_0.1_spmd.sunk | while | flops 786946 | bytes 533057 | solution.py:43
  36.3 0.2 fusion.40
  37.0 0.6 bitcast_dynamic-update-slice_fusion.2
  37.8 0.2 fusion.40
  38.2 0.2 fusion.39
  38.5 0.6 bitcast_dynamic-update-slice_fusion.2
  39.3 0.2 fusion.40
  39.7 0.2 fusion.39
  39.9 0.6 bitcast_dynamic-update-slice_fusion.2
  40.8 0.2 fusion.40
  41.4 0.6 bitcast_dynamic-update-slice_fusion.2
  42.9 0.6 bitcast_dynamic-update-slice_fusion.2
  44.4 0.6 bitcast_dynamic-update-slice_fusion.2
  45.9 0.6 bitcast_dynamic-update-slice_fusion.2
  47.3 0.6 bitcast_dynamic-update-slice_fusion.2
  48.8 0.6 bitcast_dynamic-update-slice_fusion.2
  50.3 0.6 bitcast_dynamic-update-slice_fusion.2
  51.8 0.6 bitcast_dynamic-update-slice_fusion.2
  53.3 0.6 bitcast_dynamic-update-slice_fusion.2
  54.7 0.6 bitcast_dynamic-update-slice_fusion.2
  56.2 0.6 bitcast_dynamic-update-slice_fusion.2
  57.7 0.6 bitcast_dynamic-update-slice_fusion.2
  59.2 0.6 bitcast_dynamic-update-slice_fusion.2
  59.8 3.9 %all-to-all-start.1 = ((f32[16,1,2,128]{3,2,1,0:T(2,128)}), f32[16,1,2,128]{3,2,1,0:T(2,128)S(1)}, u32[]{:S(2)}, u32[]{:S(2)}) async-start(f32[16,1,2,128]{3,2,1,0:T(2,128)} %get-tuple-element.24), calls=%async_computation.1 | async-start | bytes 32768 | tf_op jit(solution)/shard_map/all_to_all | solution.py:44
  63.9 6.3 %all-to-all-done.1 = f32[16,1,2,128]{3,2,1,0:T(2,128)S(1)} async-done(((f32[16,1,2,128]{3,2,1,0:T(2,128)}), f32[16,1,2,128]{3,2,1,0:T(2,128)S(1)}, u32[]{:S(2)}, u32[]{:S(2)}) %all-to-all-start.1) | async-done | bytes 16416 | tf_op jit(solution)/shard_map/all_to_all | solution.py:44
  70.2 1.0 %fusion.12 = f32[256,128]{1,0:T(8,128)} fusion(f32[256,16]{0,1:T(8,128)S(1)} %get-tuple-element.42, f32[256,16]{0,1:T(8,128)S(1)} %get-tuple-element.41, f32[16,128]{1,0:T(8,128)S(1)} %bitcast.99, f32[16,128]{1,0:T(8,128)S(1)} %bitcast.98), kind=kOutput, calls=%fused_computation.22 | convolution fusion | flops 12603392 | bytes 180224 | tf_op jit(solution)/shard_map/dot_general | solution.py:57
  71.2 12.8 %all-to-all-start.2 = ((f32[16,16,1,128]{3,1,2,0:T(8,128)}), f32[16,16,1,128]{3,1,2,0:T(8,128)S(1)}, u32[]{:S(2)}, u32[]{:S(2)}) async-start(f32[16,16,1,128]{3,1,2,0:T(8,128)} %bitcast.24), calls=%async_computation.2 | async-start | bytes 262144 | tf_op jit(solution)/shard_map/all_to_all | solution.py:15
  84.0 9.2 %all-to-all-done.2 = f32[16,16,1,128]{3,1,2,0:T(8,128)S(1)} async-done(((f32[16,16,1,128]{3,1,2,0:T(8,128)}), f32[16,16,1,128]{3,1,2,0:T(8,128)S(1)}, u32[]{:S(2)}, u32[]{:S(2)}) %all-to-all-start.2) | async-done | bytes 131104 | tf_op jit(solution)/shard_map/all_to_all | solution.py:15
  93.2 0.6 reduce_sum.11
  93.8 0.6 copy.24
  (81 shorter events, 12.5 us)
Async XLA Ops:
  0.6 7.7 %copy-start = (f32[16,2,128]{2,1,0:T(2,128)S(1)}, f32[16,2,128]{2,1,0:T(2,128)}, u32[]{:S(2)}) copy-start(f32[16,2,128]{2,1,0:T(2,128)} %param.5) | copy-start | bytes 49156
  0.6 35.5 %all-to-all-start = ((f32[1,16,2,128,128]{4,3,2,0,1:T(8,128)}), f32[1,16,2,128,128]{4,3,2,0,1:T(8,128)S(1)}, u32[]{:S(2)}, u32[]{:S(2)}) async-start(f32[1,16,2,128,128]{4,3,2,0,1:T(8,128)} %bitcast.95), calls=%async_computation | async-start | bytes 4194304 | tf_op jit(solution)/shard_map/all_to_all | solution.py:36
  59.8 10.4 %all-to-all-start.1 = ((f32[16,1,2,128]{3,2,1,0:T(2,128)}), f32[16,1,2,128]{3,2,1,0:T(2,128)S(1)}, u32[]{:S(2)}, u32[]{:S(2)}) async-start(f32[16,1,2,128]{3,2,1,0:T(2,128)} %get-tuple-element.24), calls=%async_computation.1 | async-start | bytes 32768 | tf_op jit(solution)/shard_map/all_to_all | solution.py:44
  71.2 21.9 %all-to-all-start.2 = ((f32[16,16,1,128]{3,1,2,0:T(8,128)}), f32[16,16,1,128]{3,1,2,0:T(8,128)S(1)}, u32[]{:S(2)}, u32[]{:S(2)}) async-start(f32[16,16,1,128]{3,1,2,0:T(8,128)} %bitcast.24), calls=%async_computation.2 | async-start | bytes 262144 | tf_op jit(solution)/shard_map/all_to_all | solution.py:15
where the time goes:
time: 94.7 us; the launch traced here: 94.4 us
  waiting for transfers between devices  43.3 us (46%)
  starting transfers between devices  24.3 us (26%)
  matrix products  14.5 us (15%)
  other arithmetic  10.7 us (11%)
    all_to_all x1, waiting for transfers between devices, local(): lax.all_to_all(propagators, 'seg', split_axis=1, concat_axis=0, tiled=True)  27.8 us
    all_to_all x1, starting transfers between devices, sum_at_owner(): lax.all_to_all(pieces, axis, split_axis=0, concat_axis=0, tiled=True)  12.8 us
    dynamic_update_slice x16, other arithmetic, local(): final_vec, chain_amps = lax.scan(advance, my_src, chain_props)  9.94 us
    all_to_all x1, waiting for transfers between devices, sum_at_owner(): lax.all_to_all(pieces, axis, split_axis=0, concat_axis=0, tiled=True)  9.17 us
    all_to_all x1, starting transfers between devices, local(): lax.all_to_all(propagators, 'seg', split_axis=1, concat_axis=0, tiled=True)  7.6 us
    all_to_all x1, waiting for transfers between devices, local(): lax.all_to_all(chain_amps, 'seg', split_axis=0, concat_axis=1, tiled=True)  6.29 us
    all_to_all x1, starting transfers between devices, local(): lax.all_to_all(chain_amps, 'seg', split_axis=0, concat_axis=1, tiled=True)  3.91 us
    dot_general x16, matrix products, apply_modes(): jnp.einsum('fij,fj->fi', prop[:, 1], vec[:, 1], precision=hi)  3.57 us
  transfers between devices with their start and end apart: 3, of which 3 were waited for; matrix products, arithmetic and copies ran while one was open for 0% of the time, Pallas kernels for 0%

commit v1 on v0

v1 whole, which is shorter than its diff:
```python
import functools

import jax
import jax.numpy as jnp
import numpy as np
from jax import lax
from jax.experimental import pallas as pl
from jax.experimental.pallas import tpu as pltpu
from jax.sharding import PartitionSpec as P

MESH = pl.DeviceIdType.MESH
F32 = jnp.float32


def ring_offsets(side):
    half = side // 2
    steps = [d if d <= half else d - side for d in range(side)]
    pairs = [(dx, dy) for dx in steps for dy in steps if (dx, dy) != (0, 0)]
    return sorted(pairs, key=lambda p: -(abs(p[0]) + abs(p[1])))


def kernel(n_seg, n_freq, prop, src, amp_out, wave_out, mats, own, amp, part, got, table,
           psend, precv, asend, arecv, wsend, wrecv, local_sem):
    side = 4
    seg = lax.axis_index("seg")
    freq = lax.axis_index("freq")
    modes = mats.shape[-1]
    rows = wave_out.shape[0]
    n_time = rows * n_freq
    x0, y0 = seg // side, lax.rem(seg, side)

    barrier = pltpu.get_barrier_semaphore()
    for k in range(1, n_seg):
        pl.semaphore_signal(barrier, 1, device_id=(freq, lax.rem(seg + k, n_seg)), device_id_type=MESH)
    for k in range(1, n_freq):
        pl.semaphore_signal(barrier, 1, device_id=(lax.rem(freq + k, n_freq), seg), device_id_type=MESH)

    keep = pltpu.make_async_copy(prop.at[0, seg], mats.at[seg], precv.at[seg])
    keep.start()
    t = lax.broadcasted_iota(jnp.int32, (n_time, n_seg), 0)
    f = lax.broadcasted_iota(jnp.int32, (n_time, n_seg), 1) + freq * n_seg
    phase = lax.rem(t * f, n_time).astype(F32) * (2.0 * np.pi / n_time)
    scale = 1.0 / np.sqrt(np.float32(n_time))
    table[0] = jnp.cos(phase) * scale
    table[1] = jnp.sin(phase) * -scale

    pl.semaphore_wait(barrier, n_seg + n_freq - 2)

    sends = []
    for i, (dx, dy) in enumerate(ring_offsets(side)):
        to = lax.rem(x0 + dx + side, side) * side + lax.rem(y0 + dy + side, side)
        copy = pltpu.make_async_remote_copy(
            prop.at[0, to], mats.at[seg], psend.at[i], precv.at[seg],
            device_id=(freq, to), device_id_type=MESH)
        copy.start()
        sends.append(copy)

    eye = lax.broadcasted_iota(jnp.int32, (modes, modes), 0) == lax.broadcasted_iota(
        jnp.int32, (modes, modes), 1)

    def to_row(column):
        return jnp.sum(jnp.where(eye, column, 0.0), axis=0, keepdims=True)

    def amp_copy(s):
        return pltpu.make_async_remote_copy(
            own.at[s], amp.at[seg], asend.at[s], arecv,
            device_id=(freq, s), device_id_type=MESH)

    def step(s, vec):
        re, im = vec
        pltpu.make_async_copy(mats.at[s], mats.at[s], precv.at[s]).wait()
        p_re, p_im = mats[s, 0], mats[s, 1]
        n_re = to_row(jnp.sum(p_re * re - p_im * im, axis=1, keepdims=True))
        n_im = to_row(jnp.sum(p_re * im + p_im * re, axis=1, keepdims=True))
        own[s, 0:1, :] = n_re
        own[s, 1:2, :] = n_im

        @pl.when(s == seg)
        def _():
            amp[s, 0:1, :] = n_re
            amp[s, 1:2, :] = n_im

        @pl.when(s != seg)
        def _():
            amp_copy(s).start()

        return n_re, n_im

    lax.fori_loop(0, n_seg, step, (src[seg, 0:1, :], src[seg, 1:2, :]))

    pltpu.make_async_copy(amp.at[pl.ds(0, n_seg - 1)], amp.at[pl.ds(0, n_seg - 1)], arecv).wait()
    amp_out[0] = amp[...]
    a_re, a_im = amp[:, 0, :], amp[:, 1, :]
    hi = lax.Precision.HIGHEST
    part[...] = (
        jnp.dot(table[0], a_re, precision=hi, preferred_element_type=F32)
        + jnp.dot(table[1], a_im, precision=hi, preferred_element_type=F32)
    ).reshape(n_freq, rows, modes)

    outs = []
    for k in range(1, n_freq):
        to = lax.rem(freq + k, n_freq)
        copy = pltpu.make_async_remote_copy(
            part.at[to], got.at[k - 1], wsend.at[k - 1], wrecv,
            device_id=(to, seg), device_id_type=MESH)
        copy.start()
        outs.append(copy)
    pltpu.make_async_copy(got, got, wrecv).wait()
    wave_out[:, 0, :] = part[freq] + jnp.sum(got[...], axis=0)

    for copy in sends:
        copy.wait_send()
    for copy in outs:
        copy.wait_send()

    def drain(s, carry):
        @pl.when(s != seg)
        def _():
            amp_copy(s).wait_send()

        return carry

    lax.fori_loop(0, n_seg, drain, 0)


def local(propagators, source_modes):
    n_seg, n_freq = lax.axis_size("seg"), lax.axis_size("freq")
    _, group, _, modes, _ = propagators.shape
    vmem = pl.BlockSpec(memory_space=pltpu.VMEM)
    dma = pltpu.SemaphoreType.DMA
    return pl.pallas_call(
        functools.partial(kernel, n_seg, n_freq),
        out_shape=(
            jax.ShapeDtypeStruct((1, group, 2, modes), F32),
            jax.ShapeDtypeStruct((group, 1, modes), F32),
        ),
        in_specs=[pl.BlockSpec(memory_space=pl.ANY), vmem],
        out_specs=(vmem, vmem),
        scratch_shapes=[
            pltpu.VMEM((n_seg, 2, modes, modes), F32),
            pltpu.VMEM((n_seg, 2, modes), F32),
            pltpu.VMEM((n_seg, 2, modes), F32),
            pltpu.VMEM((n_freq, group, modes), F32),
            pltpu.VMEM((n_freq - 1, group, modes), F32),
            pltpu.VMEM((2, n_freq * group, n_seg), F32),
            dma((n_seg - 1,)),
            dma((n_seg,)),
            dma((n_seg,)),
            dma,
            dma((n_freq - 1,)),
            dma,
            dma,
        ],
        compiler_params=pltpu.CompilerParams(
            collective_id=0, has_side_effects=True, vmem_limit_bytes=48 << 20
        ),
    )(propagators, source_modes)


def solution(mesh):
    placed = (P("seg", "freq", None, None, None), P("freq", None, None))
    return jax.shard_map(
        local,
        mesh=mesh,
        in_specs=placed,
        out_specs=(P("seg", "freq", None, None), P("freq", "seg", None)),
        check_vma=False,
    )
```

time: 94.7 us -> 52.4 us (0.55)
  Pallas kernels: 0 us -> 47.4 us
  waiting for transfers between devices: 43.3 us -> 0 us
  starting transfers between devices: 24.3 us -> 0 us
  matrix products: 14.5 us -> 0 us
  other arithmetic: 10.7 us -> 0 us
  local copies, waits for them, and re-layouts: 0.79 us -> 3.51 us
    pallas_call x0 -> x1, Pallas kernels: none -> 47.4 us  [local(): pl.pallas_call(functools.partial(kernel, n_seg, n_freq), out_shape=(jax.S...]
    all_to_all x3 -> x0, waiting for transfers between devices: 43.3 us -> none  [the longest x1 27.8 us: local(): lax.all_to_all(propagators, 'seg', split_axis=1, concat_axis=0, tiled=True)]
    all_to_all x3 -> x0, starting transfers between devices: 24.3 us -> none  [the longest x1 12.8 us: sum_at_owner(): lax.all_to_all(pieces, axis, split_axis=0, concat_axis=0, tiled=True)]
    dot_general x65 -> x0, matrix products: 14.5 us -> none  [the longest x16 3.57 us: apply_modes(): jnp.einsum('fij,fj->fi', prop[:, 1], vec[:, 1], precision=hi)]
    dynamic_update_slice x16 -> x0, other arithmetic: 9.94 us -> none  [local(): final_vec, chain_amps = lax.scan(advance, my_src, chain_props)]
    unnamed x3 -> x6, local copies, waits for them, and re-layouts: 0.61 us -> 3.51 us
  transfers between devices with their start and end apart: 3 -> 0, of which waited for: 3 -> 0; matrix products, arithmetic and copies ran while one was open for 0% -> 0% of each run, Pallas kernels for 0% -> 0%
where the time goes in v1:
time: 52.4 us; the launch traced here: 51.5 us
  Pallas kernels  47.4 us (90%)
  local copies, waits for them, and re-layouts  3.51 us (7%)
  between operations  0.65 us (1%)
    pallas_call x1, Pallas kernels, local(): pl.pallas_call(functools.partial(kernel, n_seg, n_freq), out_shape=(jax.S...  47.4 us
    unnamed x6, local copies, waits for them, and re-layouts  3.51 us

profile of v1, /device:TPU:1, one launch (start us, length us, event | category | flops | bytes accessed | tf_op | source)
XLA Modules:
  0.0 51.5 jit_solution(2660188900507171278)
XLA Ops:
  0.6 0.0 copy-start
  0.6 1.6 %copy-done = f32[1,16,2,128,128]{4,3,2,1,0:T(8,128)S(1)} copy-done((f32[1,16,2,128,128]{4,3,2,1,0:T(8,128)S(1)}, f32[1,16,2,128,128]{4,3,2,1,0:T(8,128)}, u32[]{:S(2)}) %copy-start) | copy-done | bytes 2097176
  2.2 0.0 copy-start.1
  2.2 0.7 %copy-done.1 = f32[16,2,128]{2,1,0:T(2,128)S(1)} copy-done((f32[16,2,128]{2,1,0:T(2,128)S(1)}, f32[16,2,128]{2,1,0:T(2,128)}, u32[]{:S(2)}) %copy-start.1) | copy-done | bytes 16408
  2.9 47.4 %shard_map.41 = (f32[1,16,2,128]{3,2,1,0:T(2,128)S(1)}, f32[16,1,128]{2,1,0:T(1,128)S(1)}) custom-call(f32[1,16,2,128,128]{4,3,2,1,0:T(8,128)S(1)} %copy-done, f32[16,2,128]{2,1,0:T(2,128)S(1)} %copy-done.1), custom_call_target="tpu_custom_call" | custom-call | tf_op jit(solution)/shard_map/pallas_call | solution.py:131
  50.3 0.6 %copy.6 = f32[1,16,2,128]{3,2,1,0:T(2,128)} copy(f32[1,16,2,128]{3,2,1,0:T(2,128)S(1)} %get-tuple-element.4) | data formatting | bytes 32768
  50.9 0.6 %copy.7 = f32[16,1,128]{2,1,0:T(1,128)} copy(f32[16,1,128]{2,1,0:T(1,128)S(1)} %get-tuple-element.5) | data formatting | bytes 16384
Async XLA Ops:
  0.6 1.6 %copy-start = (f32[1,16,2,128,128]{4,3,2,1,0:T(8,128)S(1)}, f32[1,16,2,128,128]{4,3,2,1,0:T(8,128)}, u32[]{:S(2)}) copy-start(f32[1,16,2,128,128]{4,3,2,1,0:T(8,128)} %prop.1) | copy-start | bytes 6291460
  2.2 0.7 %copy-start.1 = (f32[16,2,128]{2,1,0:T(2,128)S(1)}, f32[16,2,128]{2,1,0:T(2,128)}, u32[]{:S(2)}) copy-start(f32[16,2,128]{2,1,0:T(2,128)} %src.1) | copy-start | bytes 49156

commit v2 on v1

v2 whole, which is shorter than its diff:
```python
import functools

import jax
import jax.numpy as jnp
import numpy as np
from jax import lax
from jax.experimental import pallas as pl
from jax.experimental.pallas import tpu as pltpu
from jax.sharding import PartitionSpec as P

MESH = pl.DeviceIdType.MESH
F32 = jnp.float32
BF16 = jnp.bfloat16
SIDE = 4
CORES = 2
PLANE = (
    (2, 2), (1, 2), (2, 1), (-1, 2), (2, -1), (1, 1), (-1, -1), (1, -1), (-1, 1),
    (2, 0), (0, 2), (1, 0), (0, 1), (-1, 0), (0, -1),
)
PIECES = 4


def split3(value):
    hi = value.astype(BF16)
    rest = value - hi.astype(F32)
    mid = rest.astype(BF16)
    return hi, mid, (rest - mid.astype(F32)).astype(BF16)


def kernel(n_seg, n_freq, prop, src, amp_out, wave_out, mats, own, amp, part, got, table, first,
           psend, precv, asend, arecv, wsend, wrecv, fsem, line_sem):
    seg = lax.axis_index("seg")
    freq = lax.axis_index("freq")
    modes = mats.shape[-1]
    rows = wave_out.shape[0]
    n_time = rows * n_freq
    x0, y0 = seg // SIDE, lax.rem(seg, SIDE)
    depth = n_freq // CORES
    z0, core = freq // CORES, lax.rem(freq, CORES)

    def at(offset):
        dx, dy = offset
        return lax.rem(x0 + dx + SIDE, SIDE) * SIDE + lax.rem(y0 + dy + SIDE, SIDE)

    def along(dz, dc):
        return lax.rem(z0 + dz + depth, depth) * CORES + lax.rem(core + dc, CORES)

    plane = [at(offset) for offset in PLANE]
    near_line = [along(0, 1), along(1, 0), along(-1, 0)]

    barrier = pltpu.get_barrier_semaphore()
    for to in plane:
        pl.semaphore_signal(barrier, 1, device_id=(freq, to), device_id_type=MESH)
    for to in near_line:
        pl.semaphore_signal(barrier, 1, device_id=(to, seg), device_id_type=MESH)

    keep = pltpu.make_async_copy(prop.at[0, seg], mats.at[seg], precv.at[seg])
    keep.start()
    begin = pltpu.make_async_copy(src.at[seg], first, fsem)
    begin.start()

    pl.semaphore_wait(barrier, len(plane) + len(near_line))

    length = modes // PIECES
    for p in range(PIECES):
        for to in plane:
            cut = pl.ds(p * length, length)
            pltpu.make_async_remote_copy(
                prop.at[0, to, :, cut], mats.at[seg, :, cut], psend, precv.at[seg],
                device_id=(freq, to), device_id_type=MESH).start()

    width = CORES * n_seg
    t = lax.broadcasted_iota(jnp.int32, (n_time, modes), 0)
    lane = lax.broadcasted_iota(jnp.int32, (n_time, modes), 1)
    column, block = lax.rem(lane, width), lane // width
    f = column // 2 + freq * n_seg
    phase = lax.rem(t * f, n_time).astype(F32) * (2.0 * np.pi / n_time)
    scale = 1.0 / np.sqrt(np.float32(n_time))
    twiddle = jnp.where(lax.rem(column, 2) == 0, jnp.cos(phase), -jnp.sin(phase)) * scale
    t_hi, t_mid, t_lo = (v.astype(F32) for v in split3(twiddle))
    zero = jnp.zeros_like(twiddle)
    table[:, :modes] = jnp.where(block < 2, t_hi, t_mid).astype(BF16)
    table[:, modes:] = jnp.where(
        block == 0, t_hi, jnp.where(block == 1, t_lo, zero)).astype(BF16)

    rounds = depth // 2
    for r in range(rounds):
        for to in near_line:
            pl.semaphore_signal(line_sem.at[r], 1, device_id=(to, seg), device_id_type=MESH)
        pl.semaphore_wait(line_sem.at[r], len(near_line))

    eye = lax.broadcasted_iota(jnp.int32, (modes, modes), 0) == lax.broadcasted_iota(
        jnp.int32, (modes, modes), 1)

    def to_row(value):
        return jnp.sum(jnp.where(eye, value, 0.0), axis=0, keepdims=True)

    def amp_copy(s):
        return pltpu.make_async_remote_copy(
            own.at[s], amp.at[seg], asend.at[s], arecv,
            device_id=(freq, s), device_id_type=MESH)

    def step(s, vec):
        re, im = vec
        pltpu.make_async_copy(mats.at[s], mats.at[s], precv.at[s]).wait()
        p_re, p_im = mats[s, 0], mats[s, 1]
        n_re = to_row(jnp.sum(p_re * re - p_im * im, axis=1, keepdims=True))
        n_im = to_row(jnp.sum(p_re * im + p_im * re, axis=1, keepdims=True))
        own[s, 0:1, :] = n_re
        own[s, 1:2, :] = n_im

        @pl.when(s == seg)
        def _():
            amp[s, 0:1, :] = n_re
            amp[s, 1:2, :] = n_im

        @pl.when(s != seg)
        def _():
            amp_copy(s).start()

        return n_re, n_im

    begin.wait()
    lax.fori_loop(0, n_seg, step, (first[0:1, :], first[1:2, :]))

    pltpu.make_async_copy(amp.at[pl.ds(0, n_seg - 1)], amp.at[pl.ds(0, n_seg - 1)], arecv).wait()
    a_hi, a_mid, a_lo = split3(amp[...].reshape(2 * n_seg, modes))
    none = jnp.zeros_like(a_hi)
    stacked = jnp.concatenate([a_hi, a_mid, a_hi, a_mid, a_lo, a_hi, none, none], axis=0)
    part[...] = jnp.dot(table[...], stacked, preferred_element_type=F32).reshape(
        n_freq, rows, modes)

    outs = []
    half = depth // 2
    for dz in sorted(range(1 - half, half + 1), key=lambda d: -abs(d)):
        for dc in range(CORES):
            if (dz, dc) == (0, 0):
                continue
            to = along(dz, dc)
            i = len(outs)
            copy = pltpu.make_async_remote_copy(
                part.at[to], got.at[i], wsend.at[i], wrecv,
                device_id=(to, seg), device_id_type=MESH)
            copy.start()
            outs.append(copy)

    amp_out[0] = amp[...]
    sent = mats.at[pl.ds(0, n_seg - 1)]
    pltpu.make_async_copy(sent, sent, psend).wait()

    def drain(s, carry):
        @pl.when(s != seg)
        def _():
            amp_copy(s).wait_send()

        return carry

    lax.fori_loop(0, n_seg, drain, 0)
    pltpu.make_async_copy(got, got, wrecv).wait()
    wave_out[:, 0, :] = part[freq] + jnp.sum(got[...], axis=0)
    for copy in outs:
        copy.wait_send()


def local(propagators, source_modes):
    n_seg, n_freq = lax.axis_size("seg"), lax.axis_size("freq")
    _, group, _, modes, _ = propagators.shape
    dma, plain = pltpu.SemaphoreType.DMA, pltpu.SemaphoreType.REGULAR
    amps, waves = pl.pallas_call(
        functools.partial(kernel, n_seg, n_freq),
        out_shape=(
            jax.ShapeDtypeStruct((1, group, 2, modes), F32),
            jax.ShapeDtypeStruct((group, 1, modes), F32),
        ),
        in_specs=[pl.BlockSpec(memory_space=pltpu.HBM)] * 2,
        out_specs=(pl.BlockSpec(memory_space=pltpu.VMEM),) * 2,
        scratch_shapes=[
            pltpu.VMEM((n_seg, 2, modes, modes), F32),
            pltpu.VMEM((n_seg, 2, modes), F32),
            pltpu.VMEM((n_seg, 2, modes), F32),
            pltpu.VMEM((n_freq, group, modes), F32),
            pltpu.VMEM((n_freq - 1, group, modes), F32),
            pltpu.VMEM((n_freq * group, 2 * modes), BF16),
            pltpu.VMEM((2, modes), F32),
            dma,
            dma((n_seg,)),
            dma((n_seg,)),
            dma,
            dma((n_freq - 1,)),
            dma,
            dma,
            plain((n_freq // CORES // 2,)),
        ],
        compiler_params=pltpu.CompilerParams(
            collective_id=0, has_side_effects=True, vmem_limit_bytes=54500 << 10
        ),
    )(*(pltpu.with_memory_space_constraint(v, pltpu.HBM) for v in (propagators, source_modes)))

    def hand_on(a, w, a_out, w_out):
        a_out[...] = a[...]
        w_out[...] = w[...]

    return pl.pallas_call(
        hand_on,
        out_shape=(
            jax.ShapeDtypeStruct(amps.shape, F32),
            jax.ShapeDtypeStruct(waves.shape, F32),
        ),
        compiler_params=pltpu.CompilerParams(vmem_limit_bytes=4 << 20),
    )(amps, waves)


def solution(mesh):
    placed = (P("seg", "freq", None, None, None), P("freq", None, None))
    return jax.shard_map(
        local,
        mesh=mesh,
        in_specs=placed,
        out_specs=(P("seg", "freq", None, None), P("freq", "seg", None)),
        check_vma=False,
    )
```

time: 52.4 us -> 46.8 us (0.89); the launches traced: 51.5 us -> 46.7 us
  local copies, waits for them, and re-layouts: 3.51 us -> 0 us
  Pallas kernels: 47.4 us -> 46.1 us
    unnamed x6 -> x0, local copies, waits for them, and re-layouts: 3.51 us -> none
    pallas_call x1, Pallas kernels: 47.4 us -> 45.5 us  [local(): pl.pallas_call(functools.partial(kernel, n_seg, n_freq), out_shape=(jax.S...]
    pallas_call x0 -> x1, Pallas kernels: none -> 0.61 us  [local(): pl.pallas_call(hand_on, out_shape=(jax.ShapeDtypeStruct(amps.shape, F32),...]
where the time goes in v2:
time: 46.8 us; the launch traced here: 46.7 us
  Pallas kernels  46.1 us (99%)
  between operations  0.64 us (1%)
    pallas_call x1, Pallas kernels, local(): pl.pallas_call(functools.partial(kernel, n_seg, n_freq), out_shape=(jax.S...  45.5 us

profile of v2, /device:TPU:1, one launch (start us, length us, event | category | flops | bytes accessed | tf_op | source)
XLA Modules:
  0.0 46.7 jit_solution(17729066396351777723)
XLA Ops:
  0.6 45.5 %shard_map.41 = (f32[1,16,2,128]{3,2,1,0:T(2,128)S(1)}, f32[16,1,128]{2,1,0:T(1,128)S(1)}) custom-call(f32[1,16,2,128,128]{4,3,2,1,0:T(8,128)} %prop.1, f32[16,2,128]{2,1,0:T(2,128)} %src.1), custom_call_target="tpu_custom_call" | custom-call | tf_op jit(solution)/shard_map/pallas_call | solution.py:169
  46.1 0.6 %shard_map.42 = (f32[1,16,2,128]{3,2,1,0:T(2,128)}, f32[16,1,128]{2,1,0:T(1,128)}) custom-call(f32[1,16,2,128]{3,2,1,0:T(2,128)S(1)} %get-tuple-element.4.a, f32[16,1,128]{2,1,0:T(1,128)S(1)} %get-tuple-element.5.w), custom_call_target="tpu_custom_call" | custom-call | tf_op jit(solution)/shard_map/pallas_call | solution.py:203

commit v3 on v2

--- a/solution.py
+++ b/solution.py
@@ -17,7 +17,8 @@
     (2, 2), (1, 2), (2, 1), (-1, 2), (2, -1), (1, 1), (-1, -1), (1, -1), (-1, 1),
     (2, 0), (0, 2), (1, 0), (0, 1), (-1, 0), (0, -1),
 )
-PIECES = 4
+HEAD_NEAR = 96
+HEAD_SECOND = 64
 
 
 def split3(value):
@@ -28,7 +29,7 @@
 
 
 def kernel(n_seg, n_freq, prop, src, amp_out, wave_out, mats, own, amp, part, got, table, first,
-           psend, precv, asend, arecv, wsend, wrecv, fsem, line_sem):
+           psend, precv, asend, arecv, wsend, wrecv, fsem, line_sem, plane_sem):
     seg = lax.axis_index("seg")
     freq = lax.axis_index("freq")
     modes = mats.shape[-1]
@@ -46,10 +47,12 @@
         return lax.rem(z0 + dz + depth, depth) * CORES + lax.rem(core + dc, CORES)
 
     plane = [at(offset) for offset in PLANE]
+    n_far, n_near = 5, 4
+    near, second = plane[-n_near:], plane[n_far:-n_near]
     near_line = [along(0, 1), along(1, 0), along(-1, 0)]
 
     barrier = pltpu.get_barrier_semaphore()
-    for to in plane:
+    for to in near:
         pl.semaphore_signal(barrier, 1, device_id=(freq, to), device_id_type=MESH)
     for to in near_line:
         pl.semaphore_signal(barrier, 1, device_id=(to, seg), device_id_type=MESH)
@@ -59,15 +62,36 @@
     begin = pltpu.make_async_copy(src.at[seg], first, fsem)
     begin.start()
 
-    pl.semaphore_wait(barrier, len(plane) + len(near_line))
-
-    length = modes // PIECES
-    for p in range(PIECES):
-        for to in plane:
-            cut = pl.ds(p * length, length)
-            pltpu.make_async_remote_copy(
-                prop.at[0, to, :, cut], mats.at[seg, :, cut], psend, precv.at[seg],
-                device_id=(freq, to), device_id_type=MESH).start()
+    pl.semaphore_wait(barrier, len(near) + len(near_line))
+
+    def send(to, start, length):
+        cut = pl.ds(start, length)
+        pltpu.make_async_remote_copy(
+            prop.at[0, to, :, cut], mats.at[seg, :, cut], psend, precv.at[seg],
+            device_id=(freq, to), device_id_type=MESH).start()
+
+    def tell(devices, sem):
+        for to in devices:
+            pl.semaphore_signal(sem, 1, device_id=(freq, to), device_id_type=MESH)
+
+    tell(near, plane_sem.at[0])
+    for to in near:
+        send(to, 0, HEAD_NEAR)
+    pl.semaphore_wait(plane_sem.at[0], len(near))
+    tell(second, plane_sem.at[1])
+    for to in second:
+        send(to, 0, HEAD_SECOND)
+    pl.semaphore_wait(plane_sem.at[1], len(second))
+    half = modes // 2
+    for p in range(2):
+        for to in plane[:n_far]:
+            send(to, p * half, half)
+    if HEAD_SECOND < modes:
+        for to in second:
+            send(to, HEAD_SECOND, modes - HEAD_SECOND)
+    if HEAD_NEAR < modes:
+        for to in near:
+            send(to, HEAD_NEAR, modes - HEAD_NEAR)
 
     width = CORES * n_seg
     t = lax.broadcasted_iota(jnp.int32, (n_time, modes), 0)
@@ -190,6 +214,7 @@
             dma,
             dma,
             plain((n_freq // CORES // 2,)),
+            plain((2,)),
         ],
         compiler_params=pltpu.CompilerParams(
             collective_id=0, has_side_effects=True, vmem_limit_bytes=54500 << 10

time: 46.8 us -> 44.8 us (0.957); the launches traced: 46.7 us -> 44 us
  Pallas kernels: 46.1 us -> 43.3 us
    pallas_call x1, Pallas kernels: 45.5 us -> 42.7 us  [local(): pl.pallas_call(functools.partial(kernel, n_seg, n_freq), out_shape=(jax.S...]
where the time goes in v3:
time: 44.8 us; the launch traced here: 44 us
  Pallas kernels  43.3 us (97%)
  between operations  0.64 us (1%)
    pallas_call x1, Pallas kernels, local(): pl.pallas_call(functools.partial(kernel, n_seg, n_freq), out_shape=(jax.S...  42.7 us

profile of v3, /device:TPU:1, one launch (start us, length us, event | category | flops | bytes accessed | tf_op | source)
XLA Modules:
  0.0 44.0 jit_solution(17704606774919144928)
XLA Ops:
  0.6 42.7 %shard_map.41 = (f32[1,16,2,128]{3,2,1,0:T(2,128)S(1)}, f32[16,1,128]{2,1,0:T(1,128)S(1)}) custom-call(f32[1,16,2,128,128]{4,3,2,1,0:T(8,128)} %prop.1, f32[16,2,128]{2,1,0:T(2,128)} %src.1), custom_call_target="tpu_custom_call" | custom-call | tf_op jit(solution)/shard_map/pallas_call | solution.py:193
  43.3 0.6 %shard_map.42 = (f32[1,16,2,128]{3,2,1,0:T(2,128)}, f32[16,1,128]{2,1,0:T(1,128)}) custom-call(f32[1,16,2,128]{3,2,1,0:T(2,128)S(1)} %get-tuple-element.4.a, f32[16,1,128]{2,1,0:T(1,128)S(1)} %get-tuple-element.5.w), custom_call_target="tpu_custom_call" | custom-call | tf_op jit(solution)/shard_map/pallas_call | solution.py:228

commit v4 on v3

--- a/solution.py
+++ b/solution.py
@@ -124,28 +124,37 @@
             own.at[s], amp.at[seg], asend.at[s], arecv,
             device_id=(freq, s), device_id_type=MESH)
 
-    def step(s, vec):
-        re, im = vec
+    def fetch(s):
         pltpu.make_async_copy(mats.at[s], mats.at[s], precv.at[s]).wait()
-        p_re, p_im = mats[s, 0], mats[s, 1]
-        n_re = to_row(jnp.sum(p_re * re - p_im * im, axis=1, keepdims=True))
-        n_im = to_row(jnp.sum(p_re * im + p_im * re, axis=1, keepdims=True))
-        own[s, 0:1, :] = n_re
-        own[s, 1:2, :] = n_im
+        return mats[s, 0], mats[s, 1]
+
+    def give(s, re, im):
+        own[s, 0:1, :] = re
+        own[s, 1:2, :] = im
 
         @pl.when(s == seg)
         def _():
-            amp[s, 0:1, :] = n_re
-            amp[s, 1:2, :] = n_im
+            amp[s, 0:1, :] = re
+            amp[s, 1:2, :] = im
 
         @pl.when(s != seg)
         def _():
             amp_copy(s).start()
 
-        return n_re, n_im
+    def step(k, vec):
+        re, im = vec
+        p_re, p_im = fetch(2 * k)
+        c_re = jnp.sum(p_re * re - p_im * im, axis=1, keepdims=True)
+        c_im = jnp.sum(p_re * im + p_im * re, axis=1, keepdims=True)
+        give(2 * k, to_row(c_re), to_row(c_im))
+        q_re, q_im = (v.T for v in fetch(2 * k + 1))
+        re = jnp.sum(q_re * c_re - q_im * c_im, axis=0, keepdims=True)
+        im = jnp.sum(q_re * c_im + q_im * c_re, axis=0, keepdims=True)
+        give(2 * k + 1, re, im)
+        return re, im
 
     begin.wait()
-    lax.fori_loop(0, n_seg, step, (first[0:1, :], first[1:2, :]))
+    lax.fori_loop(0, n_seg // 2, step, (first[0:1, :], first[1:2, :]))
 
     pltpu.make_async_copy(amp.at[pl.ds(0, n_seg - 1)], amp.at[pl.ds(0, n_seg - 1)], arecv).wait()
     a_hi, a_mid, a_lo = split3(amp[...].reshape(2 * n_seg, modes))

time: 44.8 us -> 44.7 us (level)
  no operation moved by 1% of the time
where the time goes in v4:
time: 44.7 us; the launch traced here: 44 us
  Pallas kernels  43.3 us (97%)
  between operations  0.64 us (1%)
    pallas_call x1, Pallas kernels, local(): pl.pallas_call(functools.partial(kernel, n_seg, n_freq), out_shape=(jax.S...  42.7 us

profile of v4, /device:TPU:1, one launch (start us, length us, event | category | flops | bytes accessed | tf_op | source)
XLA Modules:
  0.0 44.0 jit_solution(11551746460604826250)
XLA Ops:
  0.6 42.7 %shard_map.41 = (f32[1,16,2,128]{3,2,1,0:T(2,128)S(1)}, f32[16,1,128]{2,1,0:T(1,128)S(1)}) custom-call(f32[1,16,2,128,128]{4,3,2,1,0:T(8,128)} %prop.1, f32[16,2,128]{2,1,0:T(2,128)} %src.1), custom_call_target="tpu_custom_call" | custom-call | tf_op jit(solution)/shard_map/pallas_call | solution.py:202
  43.3 0.6 %shard_map.42 = (f32[1,16,2,128]{3,2,1,0:T(2,128)}, f32[16,1,128]{2,1,0:T(1,128)}) custom-call(f32[1,16,2,128]{3,2,1,0:T(2,128)S(1)} %get-tuple-element.4.a, f32[16,1,128]{2,1,0:T(1,128)S(1)} %get-tuple-element.5.w), custom_call_target="tpu_custom_call" | custom-call | tf_op jit(solution)/shard_map/pallas_call | solution.py:237

commit v5 on v4

--- a/solution.py
+++ b/solution.py
@@ -17,6 +17,7 @@
     (2, 2), (1, 2), (2, 1), (-1, 2), (2, -1), (1, 1), (-1, -1), (1, -1), (-1, 1),
     (2, 0), (0, 2), (1, 0), (0, 1), (-1, 0), (0, -1),
 )
+DIRECT = 48
 HEAD_NEAR = 96
 HEAD_SECOND = 64
 
@@ -29,7 +30,8 @@
 
 
 def kernel(n_seg, n_freq, prop, src, amp_out, wave_out, mats, own, amp, part, got, table, first,
-           psend, precv, asend, arecv, wsend, wrecv, fsem, line_sem, plane_sem):
+           psend, precv, asend, arecv, wsend, wrecv, fsem, line_sem, plane_sem, relay,
+           relay_send, relay_recv, hello, ask, go):
     seg = lax.axis_index("seg")
     freq = lax.axis_index("freq")
     modes = mats.shape[-1]
@@ -50,19 +52,43 @@
     n_far, n_near = 5, 4
     near, second = plane[-n_near:], plane[n_far:-n_near]
     near_line = [along(0, 1), along(1, 0), along(-1, 0)]
+    middle = depth // 2
+    late = z0 >= middle
+    helps = z0 < middle - 1
+    helps_two = z0 == 0
+    slot = jnp.where(z0 == middle, 1, 0)
+    helper = jnp.where(z0 == middle, 0, depth - 1 - z0) * CORES + core
+    clients = ((depth - 1 - z0) * CORES + core, middle * CORES + core)
 
     barrier = pltpu.get_barrier_semaphore()
+
+    def greet(line, plane_to):
+        pl.semaphore_signal(barrier, 1, device_id=(line, plane_to), device_id_type=MESH)
+
     for to in near:
-        pl.semaphore_signal(barrier, 1, device_id=(freq, to), device_id_type=MESH)
-    for to in near_line:
-        pl.semaphore_signal(barrier, 1, device_id=(to, seg), device_id_type=MESH)
+        greet(freq, to)
+    greet(along(0, 1), seg)
+
+    @pl.when(z0 < depth - 1)
+    def _():
+        greet(along(1, 0), seg)
+
+    @pl.when(helps)
+    def _():
+        greet(clients[0], seg)
+
+    @pl.when(helps_two)
+    def _():
+        greet(clients[1], seg)
 
     keep = pltpu.make_async_copy(prop.at[0, seg], mats.at[seg], precv.at[seg])
     keep.start()
     begin = pltpu.make_async_copy(src.at[seg], first, fsem)
     begin.start()
 
-    pl.semaphore_wait(barrier, len(near) + len(near_line))
+    below = jnp.where(z0 > 0, 1, 0)
+    is_late = jnp.where(late, 1, 0)
+    pl.semaphore_wait(barrier, len(near) + 1 + below + is_late)
 
     def send(to, start, length):
         cut = pl.ds(start, length)
@@ -74,9 +100,41 @@
         for to in devices:
             pl.semaphore_signal(sem, 1, device_id=(freq, to), device_id_type=MESH)
 
+    def send_farthest(p, length):
+        @pl.when(jnp.logical_not(late))
+        def _():
+            send(plane[0], p * length, length)
+
+        if DIRECT > p * length:
+            @pl.when(late)
+            def _():
+                send(plane[0], p * length, min(length, DIRECT - p * length))
+
+    def send_relayed():
+        @pl.when(late)
+        def _():
+            pl.semaphore_wait(go, 1)
+            cut = pl.ds(DIRECT, modes - DIRECT)
+            pltpu.make_async_remote_copy(
+                prop.at[0, plane[0], :, cut], relay.at[slot], psend, relay_recv.at[slot],
+                device_id=(helper, plane[0]), device_id_type=MESH).start()
+
     tell(near, plane_sem.at[0])
     for to in near:
         send(to, 0, HEAD_NEAR)
+    @pl.when(z0 > 0)
+    def _():
+        pl.semaphore_signal(hello, 1, device_id=(along(-1, 0), seg), device_id_type=MESH)
+
+    @pl.when(late)
+    def _():
+        pl.semaphore_signal(ask, 1, device_id=(helper, seg), device_id_type=MESH)
+
+    @pl.when(z0 == depth - 1)
+    def _():
+        pl.semaphore_signal(hello, 1, device_id=(along(1, 0), seg), device_id_type=MESH)
+
+
     pl.semaphore_wait(plane_sem.at[0], len(near))
     tell(second, plane_sem.at[1])
     for to in second:
@@ -84,14 +142,35 @@
     pl.semaphore_wait(plane_sem.at[1], len(second))
     half = modes // 2
     for p in range(2):
-        for to in plane[:n_far]:
+        send_farthest(p, half)
+        for to in plane[1:n_far]:
             send(to, p * half, half)
+        if p == 0:
+            send_relayed()
     if HEAD_SECOND < modes:
         for to in second:
             send(to, HEAD_SECOND, modes - HEAD_SECOND)
     if HEAD_NEAR < modes:
         for to in near:
             send(to, HEAD_NEAR, modes - HEAD_NEAR)
+
+    forward = [
+        pltpu.make_async_remote_copy(
+            relay.at[i], mats.at[plane[0], :, pl.ds(DIRECT, modes - DIRECT)], relay_send.at[i],
+            precv.at[plane[0]], device_id=(client, seg), device_id_type=MESH)
+        for i, client in enumerate(clients)
+    ]
+
+    @pl.when(helps_two)
+    def _():
+        pl.semaphore_wait(ask, 2)
+        for client in clients:
+            pl.semaphore_signal(go, 1, device_id=(client, seg), device_id_type=MESH)
+
+    @pl.when(jnp.logical_and(helps, jnp.logical_not(helps_two)))
+    def _():
+        pl.semaphore_wait(ask, 1)
+        pl.semaphore_signal(go, 1, device_id=(clients[0], seg), device_id_type=MESH)
 
     width = CORES * n_seg
     t = lax.broadcasted_iota(jnp.int32, (n_time, modes), 0)
@@ -107,6 +186,20 @@
     table[:, modes:] = jnp.where(
         block == 0, t_hi, jnp.where(block == 1, t_lo, zero)).astype(BF16)
 
+    for i, here in enumerate((helps, helps_two)):
+        @pl.when(here)
+        def _(i=i):
+            pltpu.make_async_copy(relay.at[i], relay.at[i], relay_recv.at[i]).wait()
+            forward[i].start()
+
+    @pl.when(z0 == 0)
+    def _():
+        pl.semaphore_wait(hello, 2)
+
+    @pl.when(jnp.logical_and(z0 > 0, z0 < depth - 1))
+    def _():
+        pl.semaphore_wait(hello, 1)
+
     rounds = depth // 2
     for r in range(rounds):
         for to in near_line:
@@ -193,6 +286,11 @@
     wave_out[:, 0, :] = part[freq] + jnp.sum(got[...], axis=0)
     for copy in outs:
         copy.wait_send()
+
+    for i, here in enumerate((helps, helps_two)):
+        @pl.when(here)
+        def _(i=i):
+            forward[i].wait_send()
 
 
 def local(propagators, source_modes):
@@ -224,6 +322,12 @@
             dma,
             plain((n_freq // CORES // 2,)),
             plain((2,)),
+            pltpu.VMEM((2, 2, modes - DIRECT, modes), F32),
+            dma((2,)),
+            dma((2,)),
+            plain,
+            plain,
+            plain,
         ],
         compiler_params=pltpu.CompilerParams(
             collective_id=0, has_side_effects=True, vmem_limit_bytes=54500 << 10

time: 44.7 us -> 43 us (0.962); the launches traced: 44 us -> 42.8 us
  Pallas kernels: 43.3 us -> 42.1 us
    pallas_call x1, Pallas kernels: 42.7 us -> 41.5 us  [local(): pl.pallas_call(functools.partial(kernel, n_seg, n_freq), out_shape=(jax.S...]
where the time goes in v5:
time: 43 us; the launch traced here: 42.8 us
  Pallas kernels  42.1 us (98%)
  between operations  0.64 us (1%)
    pallas_call x1, Pallas kernels, local(): pl.pallas_call(functools.partial(kernel, n_seg, n_freq), out_shape=(jax.S...  41.5 us

profile of v5, /device:TPU:1, one launch (start us, length us, event | category | flops | bytes accessed | tf_op | source)
XLA Modules:
  0.0 42.8 jit_solution(7513102155939481701)
XLA Ops:
  0.6 41.5 %shard_map.41 = (f32[1,16,2,128]{3,2,1,0:T(2,128)S(1)}, f32[16,1,128]{2,1,0:T(1,128)S(1)}) custom-call(f32[1,16,2,128,128]{4,3,2,1,0:T(8,128)} %prop.1, f32[16,2,128]{2,1,0:T(2,128)} %src.1), custom_call_target="tpu_custom_call" | custom-call | tf_op jit(solution)/shard_map/pallas_call | solution.py:300
  42.1 0.6 %shard_map.42 = (f32[1,16,2,128]{3,2,1,0:T(2,128)}, f32[16,1,128]{2,1,0:T(1,128)}) custom-call(f32[1,16,2,128]{3,2,1,0:T(2,128)S(1)} %get-tuple-element.4.a, f32[16,1,128]{2,1,0:T(1,128)S(1)} %get-tuple-element.5.w), custom_call_target="tpu_custom_call" | custom-call | tf_op jit(solution)/shard_map/pallas_call | solution.py:341

commit v6 on v5

--- a/solution.py
+++ b/solution.py
@@ -37,13 +37,15 @@
     modes = mats.shape[-1]
     rows = wave_out.shape[0]
     n_time = rows * n_freq
-    x0, y0 = seg // SIDE, lax.rem(seg, SIDE)
+    x0, y0 = lax.div(seg, SIDE), lax.rem(seg, SIDE)
     depth = n_freq // CORES
-    z0, core = freq // CORES, lax.rem(freq, CORES)
+    z0, core = lax.div(freq, CORES), lax.rem(freq, CORES)
+    across = {d: lax.rem(x0 + d + SIDE, SIDE) * SIDE for d in (1, -1, 2)} | {0: x0 * SIDE}
+    down = {d: lax.rem(y0 + d + SIDE, SIDE) for d in (1, -1, 2)} | {0: y0}
 
     def at(offset):
         dx, dy = offset
-        return lax.rem(x0 + dx + SIDE, SIDE) * SIDE + lax.rem(y0 + dy + SIDE, SIDE)
+        return across[dx] + down[dy]
 
     def along(dz, dc):
         return lax.rem(z0 + dz + depth, depth) * CORES + lax.rem(core + dc, CORES)
@@ -225,11 +227,6 @@
         own[s, 0:1, :] = re
         own[s, 1:2, :] = im
 
-        @pl.when(s == seg)
-        def _():
-            amp[s, 0:1, :] = re
-            amp[s, 1:2, :] = im
-
         @pl.when(s != seg)
         def _():
             amp_copy(s).start()
@@ -248,6 +245,7 @@
 
     begin.wait()
     lax.fori_loop(0, n_seg // 2, step, (first[0:1, :], first[1:2, :]))
+    amp[seg] = own[seg]
 
     pltpu.make_async_copy(amp.at[pl.ds(0, n_seg - 1)], amp.at[pl.ds(0, n_seg - 1)], arecv).wait()
     a_hi, a_mid, a_lo = split3(amp[...].reshape(2 * n_seg, modes))

time: 43 us -> 42.9 us (level)
  no operation moved by 1% of the time
where the time goes in v6:
time: 42.9 us; the launch traced here: 42.8 us
  Pallas kernels  42.1 us (98%)
  between operations  0.64 us (1%)
    pallas_call x1, Pallas kernels, local(): pl.pallas_call(functools.partial(kernel, n_seg, n_freq), out_shape=(jax.S...  41.5 us

profile of v6, /device:TPU:1, one launch (start us, length us, event | category | flops | bytes accessed | tf_op | source)
XLA Modules:
  0.0 42.8 jit_solution(16742378450347711897)
XLA Ops:
  0.6 41.5 %shard_map.41 = (f32[1,16,2,128]{3,2,1,0:T(2,128)S(1)}, f32[16,1,128]{2,1,0:T(1,128)S(1)}) custom-call(f32[1,16,2,128,128]{4,3,2,1,0:T(8,128)} %prop.1, f32[16,2,128]{2,1,0:T(2,128)} %src.1), custom_call_target="tpu_custom_call" | custom-call | tf_op jit(solution)/shard_map/pallas_call | solution.py:298
  42.1 0.6 %shard_map.42 = (f32[1,16,2,128]{3,2,1,0:T(2,128)}, f32[16,1,128]{2,1,0:T(1,128)}) custom-call(f32[1,16,2,128]{3,2,1,0:T(2,128)S(1)} %get-tuple-element.4.a, f32[16,1,128]{2,1,0:T(1,128)S(1)} %get-tuple-element.5.w), custom_call_target="tpu_custom_call" | custom-call | tf_op jit(solution)/shard_map/pallas_call | solution.py:339

commit v7 on v6

--- a/solution.py
+++ b/solution.py
@@ -231,20 +231,16 @@
         def _():
             amp_copy(s).start()
 
-    def step(k, vec):
+    def step(s, vec):
         re, im = vec
-        p_re, p_im = fetch(2 * k)
-        c_re = jnp.sum(p_re * re - p_im * im, axis=1, keepdims=True)
-        c_im = jnp.sum(p_re * im + p_im * re, axis=1, keepdims=True)
-        give(2 * k, to_row(c_re), to_row(c_im))
-        q_re, q_im = (v.T for v in fetch(2 * k + 1))
-        re = jnp.sum(q_re * c_re - q_im * c_im, axis=0, keepdims=True)
-        im = jnp.sum(q_re * c_im + q_im * c_re, axis=0, keepdims=True)
-        give(2 * k + 1, re, im)
-        return re, im
+        p_re, p_im = fetch(s)
+        n_re = to_row(jnp.sum(p_re * re - p_im * im, axis=1, keepdims=True))
+        n_im = to_row(jnp.sum(p_re * im + p_im * re, axis=1, keepdims=True))
+        give(s, n_re, n_im)
+        return n_re, n_im
 
     begin.wait()
-    lax.fori_loop(0, n_seg // 2, step, (first[0:1, :], first[1:2, :]))
+    lax.fori_loop(0, n_seg, step, (first[0:1, :], first[1:2, :]))
     amp[seg] = own[seg]
 
     pltpu.make_async_copy(amp.at[pl.ds(0, n_seg - 1)], amp.at[pl.ds(0, n_seg - 1)], arecv).wait()

time: 42.9 us -> 43 us (level)
  no operation moved by 1% of the time
where the time goes in v7:
time: 43 us; the launch traced here: 42.8 us
  Pallas kernels  42.1 us (98%)
  between operations  0.64 us (1%)
    pallas_call x1, Pallas kernels, local(): pl.pallas_call(functools.partial(kernel, n_seg, n_freq), out_shape=(jax.S...  41.5 us

profile of v7, /device:TPU:1, one launch (start us, length us, event | category | flops | bytes accessed | tf_op | source)
XLA Modules:
  0.0 42.8 jit_solution(12375724207880388417)
XLA Ops:
  0.6 41.5 %shard_map.41 = (f32[1,16,2,128]{3,2,1,0:T(2,128)S(1)}, f32[16,1,128]{2,1,0:T(1,128)S(1)}) custom-call(f32[1,16,2,128,128]{4,3,2,1,0:T(8,128)} %prop.1, f32[16,2,128]{2,1,0:T(2,128)} %src.1), custom_call_target="tpu_custom_call" | custom-call | tf_op jit(solution)/shard_map/pallas_call | solution.py:294
  42.1 0.6 %shard_map.42 = (f32[1,16,2,128]{3,2,1,0:T(2,128)}, f32[16,1,128]{2,1,0:T(1,128)}) custom-call(f32[1,16,2,128]{3,2,1,0:T(2,128)S(1)} %get-tuple-element.4.a, f32[16,1,128]{2,1,0:T(1,128)S(1)} %get-tuple-element.5.w), custom_call_target="tpu_custom_call" | custom-call | tf_op jit(solution)/shard_map/pallas_call | solution.py:335

commit v8 on v7

--- a/solution.py
+++ b/solution.py
@@ -240,7 +240,7 @@
         return n_re, n_im
 
     begin.wait()
-    lax.fori_loop(0, n_seg, step, (first[0:1, :], first[1:2, :]))
+    lax.fori_loop(0, n_seg, step, (first[0:1, :], first[1:2, :]), unroll=2)
     amp[seg] = own[seg]
 
     pltpu.make_async_copy(amp.at[pl.ds(0, n_seg - 1)], amp.at[pl.ds(0, n_seg - 1)], arecv).wait()

time: 43 us -> 43 us (level)
  no operation moved by 1% of the time
where the time goes in v8:
time: 43 us; the launch traced here: 42.8 us
  Pallas kernels  42.1 us (98%)
  between operations  0.64 us (1%)
    pallas_call x1, Pallas kernels, local(): pl.pallas_call(functools.partial(kernel, n_seg, n_freq), out_shape=(jax.S...  41.5 us

profile of v8, /device:TPU:1, one launch (start us, length us, event | category | flops | bytes accessed | tf_op | source)
XLA Modules:
  0.0 42.8 jit_solution(11374252096236140858)
XLA Ops:
  0.6 41.5 %shard_map.41 = (f32[1,16,2,128]{3,2,1,0:T(2,128)S(1)}, f32[16,1,128]{2,1,0:T(1,128)S(1)}) custom-call(f32[1,16,2,128,128]{4,3,2,1,0:T(8,128)} %prop.1, f32[16,2,128]{2,1,0:T(2,128)} %src.1), custom_call_target="tpu_custom_call" | custom-call | tf_op jit(solution)/shard_map/pallas_call | solution.py:294
  42.1 0.6 %shard_map.42 = (f32[1,16,2,128]{3,2,1,0:T(2,128)}, f32[16,1,128]{2,1,0:T(1,128)}) custom-call(f32[1,16,2,128]{3,2,1,0:T(2,128)S(1)} %get-tuple-element.4.a, f32[16,1,128]{2,1,0:T(1,128)S(1)} %get-tuple-element.5.w), custom_call_target="tpu_custom_call" | custom-call | tf_op jit(solution)/shard_map/pallas_call | solution.py:335

commit v9 on v7

--- a/solution.py
+++ b/solution.py
@@ -143,18 +143,17 @@
         send(to, 0, HEAD_SECOND)
     pl.semaphore_wait(plane_sem.at[1], len(second))
     half = modes // 2
+    rest = (modes - HEAD_SECOND) // 2
     for p in range(2):
         send_farthest(p, half)
         for to in plane[1:n_far]:
             send(to, p * half, half)
         if p == 0:
             send_relayed()
-    if HEAD_SECOND < modes:
         for to in second:
-            send(to, HEAD_SECOND, modes - HEAD_SECOND)
-    if HEAD_NEAR < modes:
-        for to in near:
-            send(to, HEAD_NEAR, modes - HEAD_NEAR)
+            send(to, HEAD_SECOND + p * rest, rest)
+    for to in near:
+        send(to, HEAD_NEAR, modes - HEAD_NEAR)
 
     forward = [
         pltpu.make_async_remote_copy(

time: 43 us -> 43.1 us (level)
  no operation moved by 1% of the time
where the time goes in v9:
time: 43.1 us; the launch traced here: 42.9 us
  Pallas kernels  42.2 us (98%)
  between operations  0.64 us (1%)
    pallas_call x1, Pallas kernels, local(): pl.pallas_call(functools.partial(kernel, n_seg, n_freq), out_shape=(jax.S...  41.6 us

profile of v9, /device:TPU:1, one launch (start us, length us, event | category | flops | bytes accessed | tf_op | source)
XLA Modules:
  0.0 42.9 jit_solution(12310868860326275612)
XLA Ops:
  0.6 41.6 %shard_map.41 = (f32[1,16,2,128]{3,2,1,0:T(2,128)S(1)}, f32[16,1,128]{2,1,0:T(1,128)S(1)}) custom-call(f32[1,16,2,128,128]{4,3,2,1,0:T(8,128)} %prop.1, f32[16,2,128]{2,1,0:T(2,128)} %src.1), custom_call_target="tpu_custom_call" | custom-call | tf_op jit(solution)/shard_map/pallas_call | solution.py:293
  42.2 0.6 %shard_map.42 = (f32[1,16,2,128]{3,2,1,0:T(2,128)}, f32[16,1,128]{2,1,0:T(1,128)}) custom-call(f32[1,16,2,128]{3,2,1,0:T(2,128)S(1)} %get-tuple-element.4.a, f32[16,1,128]{2,1,0:T(1,128)S(1)} %get-tuple-element.5.w), custom_call_target="tpu_custom_call" | custom-call | tf_op jit(solution)/shard_map/pallas_call | solution.py:334
